TPU v7x, 32 devices: a whole 2x2x4 slice. The times are simulated.
32 devices in a mesh: row: 2 (over core), col: 4 (over y, x), depth: 4 (over z).
Axes of the slice: x: 2, y: 2, z: 4, core: 2. Of those that a mesh axis runs over, the one named last changes fastest.
Arguments:
- tokens: bfloat16 [1024, 8192], P(('col', 'depth'), 'row'), may hold values from -6 to 6
- out_grad: bfloat16 [1024, 8192], P(('col', 'depth'), 'row'), may hold values from -6 to 6
- gate_w: bfloat16 [8192, 14336], P('row', ('col', 'depth')), may hold values from -0.09375 to 0.09375
- up_w: bfloat16 [8192, 14336], P('row', ('col', 'depth')), may hold values from -0.09375 to 0.09375
- down_w: bfloat16 [14336, 8192], P(('col', 'depth'), 'row'), may hold values from -0.0625 to 0.0625
- keep_gate: int32 [64, 112], P('row', ('col', 'depth')), may hold values from 0 to 1, as said below
- keep_up: int32 [64, 112], P('row', ('col', 'depth')), may hold values from 0 to 1, as said below
- keep_down: int32 [112, 64], P(('col', 'depth'), 'row'), may hold values from 0 to 1, as said below
- exp_gate: int32 [64, 112], P('row', ('col', 'depth')), may hold values from -1 to 1
- exp_up: int32 [64, 112], P('row', ('col', 'depth')), may hold values from -1 to 1
- exp_down: int32 [112, 64], P(('col', 'depth'), 'row'), may hold values from -1 to 1
Outputs:
- output: bfloat16 [1024, 8192], P(('col', 'depth'), 'row')
- input_grad: bfloat16 [1024, 8192], P(('col', 'depth'), 'row')
- gate_w_grad: bfloat16 [8192, 14336], P('row', ('col', 'depth'))
- up_w_grad: bfloat16 [8192, 14336], P('row', ('col', 'depth'))
- down_w_grad: bfloat16 [14336, 8192], P(('col', 'depth'), 'row')
Inputs may be any that keep to these rules, and one draw needn't show every extreme that they name: `keep_gate`: 1 where a weight block is kept, 0 where it is dropped; the share kept may differ from one block column to another. `keep_up`: 1 where a weight block is kept, 0 where it is dropped; the share kept may differ from one block column to another. `keep_down`: 1 where a weight block is kept, 0 where it is dropped; the share kept may differ from one block column to another.
All inputs are finite; a program needn't handle non-finite values.
Results may differ from a plain program's by a relative error of at most 0.005.
Values may be sent and summed in bfloat16 or wider, within the bound.
A program may use at most 256 MiB of HBM per device.

v0:
```python
import jax
import jax.numpy as jnp
from jax import lax
from jax.sharding import PartitionSpec as P


def block_factor(keep, exps):
    return keep.astype(jnp.float32) * jnp.exp2(exps.astype(jnp.float32))


def scaled(raw, factor):
    rows, cols = factor.shape
    high = raw.shape[0] // rows
    wide = raw.shape[1] // cols
    blocks = raw.reshape(rows, high, cols, wide) * factor.astype(jnp.bfloat16)[:, None, :, None]
    return blocks.reshape(raw.shape)


def masked_grad(grad, factor):
    rows, cols = factor.shape
    blocks = (
        grad.reshape(rows, grad.shape[0] // rows, cols, grad.shape[1] // cols)
        * factor[:, None, :, None]
    )
    return blocks.reshape(grad.shape).astype(jnp.bfloat16)


def activate(gate, up, hidden_grad):
    sig = jax.nn.sigmoid(gate)
    hidden = (gate * sig * up).astype(jnp.bfloat16)
    gate_grad = (hidden_grad * up * sig * (1.0 + gate * (1.0 - sig))).astype(jnp.bfloat16)
    up_grad = (hidden_grad * gate * sig).astype(jnp.bfloat16)
    return (hidden, gate_grad, up_grad)


def shards(
    tokens,
    out_grad,
    gate_w,
    up_w,
    down_w,
    keep_gate,
    keep_up,
    keep_down,
    exp_gate,
    exp_up,
    exp_down,
):
    factor_gate = block_factor(keep_gate, exp_gate)
    factor_up = block_factor(keep_up, exp_up)
    factor_down = block_factor(keep_down, exp_down)
    eff_gate = scaled(gate_w, factor_gate)
    eff_up = scaled(up_w, factor_up)
    eff_down = scaled(down_w, factor_down)
    panel = gate_w.shape[0]
    width = gate_w.shape[1]
    paired = jnp.concatenate([eff_gate, eff_up], axis=1)
    gathered_in, gathered_grad = (
        lax.all_gather(tokens, ("col", "depth"), axis=0, tiled=True),
        lax.all_gather(out_grad, ("col", "depth"), axis=0, tiled=True),
    )
    sums = lax.psum_scatter(
        jnp.concatenate(
            [
                jnp.dot(gathered_in, paired, preferred_element_type=jnp.float32),
                jnp.dot(gathered_grad, eff_down.T, preferred_element_type=jnp.float32),
            ],
            axis=1,
        ),
        "row",
        scatter_dimension=0,
        tiled=True,
    )
    hidden, gate_grad, up_grad = activate(
        sums[:, :width], sums[:, width : 2 * width], sums[:, 2 * width :]
    )
    whole = lax.all_gather(
        jnp.concatenate([hidden, gate_grad, up_grad], axis=1), "row", axis=0, tiled=True
    )
    hidden_all = whole[:, :width]
    pair_grad = whole[:, width:]
    result = lax.psum_scatter(
        jnp.concatenate(
            [
                jnp.dot(hidden_all, eff_down, preferred_element_type=jnp.float32),
                jnp.dot(pair_grad, paired.T, preferred_element_type=jnp.float32),
            ],
            axis=1,
        ),
        ("col", "depth"),
        scatter_dimension=0,
        tiled=True,
    )
    output = result[:, :panel].astype(jnp.bfloat16)
    input_grad = result[:, panel:].astype(jnp.bfloat16)
    pair_weights = jnp.dot(gathered_in.T, pair_grad, preferred_element_type=jnp.float32)
    gate_w_grad = masked_grad(pair_weights[:, :width], factor_gate)
    up_w_grad = masked_grad(pair_weights[:, width:], factor_up)
    down_w_grad = masked_grad(
        jnp.dot(hidden_all.T, gathered_grad, preferred_element_type=jnp.float32), factor_down
    )
    return (output, input_grad, gate_w_grad, up_w_grad, down_w_grad)


def solution(mesh):
    return jax.shard_map(
        shards,
        mesh=mesh,
        in_specs=(
            P(("col", "depth"), "row"),
            P(("col", "depth"), "row"),
            P("row", ("col", "depth")),
            P("row", ("col", "depth")),
            P(("col", "depth"), "row"),
            P("row", ("col", "depth")),
            P("row", ("col", "depth")),
            P(("col", "depth"), "row"),
            P("row", ("col", "depth")),
            P("row", ("col", "depth")),
            P(("col", "depth"), "row"),
        ),
        out_specs=(
            P(("col", "depth"), "row"),
            P(("col", "depth"), "row"),
            P("row", ("col", "depth")),
            P("row", ("col", "depth")),
            P(("col", "depth"), "row"),
        ),
        check_vma=False,
    )
```

profile of v0, /device:TPU:0, one launch (start us, length us, event | category | flops | bytes accessed | tf_op | source)
XLA Modules:
  0.0 1067.9 jit_solution(7671832824906796205)
XLA Ops:
  7.2 0.0 all-gather.6.cloned.1.call-start
  7.2 0.7 all-gather.6.cloned.1.call-update
  7.9 0.0 all-gather.4.cloned.1.call-start
  7.9 0.7 all-gather.4.cloned.1.call-update
  8.6 0.0 reduce-scatter.3.cloned.1.call-start
  8.7 10.8 %copy.20 = bf16[4096,896]{0,1:T(8,128)(2,1)} copy(bf16[4096,896]{1,0:T(8,128)(2,1)} %param.13) | data formatting | bytes 14680064 | tf_op args[2]
  19.5 0.0 copy-start.9
  19.5 0.0 copy-start.10
  19.5 11.1 %copy.21 = bf16[4096,896]{0,1:T(8,128)(2,1)} copy(bf16[4096,896]{1,0:T(8,128)(2,1)} %param.14) | data formatting | bytes 14680064 | tf_op args[3]
  30.6 0.0 copy-done.6
  30.6 0.6 fusion.14
  31.2 0.6 fusion.15
  31.8 0.6 fusion.13
  32.4 1.0 mul.104
  33.5 4.7 mul.100
  38.2 1.7 copy-done
  39.9 10.6 bitcast_multiply_fusion.4
  50.5 75.3 %all-gather.6.cloned.1.call-done = bf16[1024,4096]{1,0:T(8,128)(2,1)} async-done(((bf16[64,4096]{1,0:T(8,128)(2,1)}), bf16[1024,4096]{1,0:T(8,128)(2,1)}) %all-gather.6.cloned.1.call-update) | async-done | bytes 8388624 | tf_op jit(solution)/shard_map/all_gather | solution.py:60
  125.8 1.0 mul.108
  126.9 2.9 copy-done.1
  129.8 16.3 %convolution_bitcast_fusion.1 = f32[1024,896]{0,1:T(8,128)} fusion(bf16[1024,4096]{1,0:T(8,128)(2,1)} %all-gather.6.cloned.1.call-done, bf16[896,4096]{1,0:T(8,128)(2,1)} %param.15, bf16[112,8,32,128]{3,2,1,0:T(8,128)(2,1)S(1)} %bitcast.54), kind=kOutput, calls=%fused_computation.19 | convolution fusion | flops 7519862784 | bytes 26738688 | tf_op jit(solution)/shard_map/dot_general | solution.py:66
  146.0 93.1 %all-gather.4.cloned.1.call-done = bf16[1024,4096]{1,0:T(8,128)(2,1)} async-done(((bf16[64,4096]{1,0:T(8,128)(2,1)}), bf16[1024,4096]{1,0:T(8,128)(2,1)}) %all-gather.4.cloned.1.call-update) | async-done | bytes 8388624 | tf_op jit(solution)/shard_map/all_gather | solution.py:59
  239.1 22.9 %fusion.5 = f32[1024,1792]{0,1:T(8,128)} fusion(bf16[1024,4096]{1,0:T(8,128)(2,1)} %all-gather.4.cloned.1.call-done, bf16[4096,896]{0,1:T(8,128)(2,1)} %get-tuple-element.28, bf16[4096,896]{0,1:T(8,128)(2,1)} %get-tuple-element.29), kind=kOutput, calls=%fused_computation.15 | convolution fusion | flops 15061745664 | bytes 30408704 | tf_op jit(solution)/shard_map/dot_general | solution.py:65
  262.0 10.7 %pad_maximum_fusion.2 = f32[1024,2688]{0,1:T(8,128)} fusion(f32[1024,896]{0,1:T(8,128)} %convolution_bitcast_fusion.1, f32[1024,1792]{0,1:T(8,128)} %fusion.5), kind=kLoop, calls=%fused_computation.9 | loop fusion | flops 2752512 | bytes 22020096 | tf_op jit(solution)/shard_map/concatenate | solution.py:63
  272.7 0.0 reduce-scatter.3.cloned.1.call-update
  272.8 0.0 all-gather.8.cloned.1.call-start
  272.8 16.5 %reduce-scatter.3.cloned.1.call-done = f32[512,2688]{0,1:T(8,128)} async-done(((f32[1024,2688]{0,1:T(8,128)}), f32[512,2688]{0,1:T(8,128)}) %reduce-scatter.3.cloned.1.call-update) | async-done | bytes 5505040 | tf_op jit(solution)/shard_map/reduce_scatter | solution.py:62
  289.3 3.7 multiply_convert_fusion.2
  293.0 1.7 pad_maximum_fusion.7
  294.8 0.0 all-gather.8.cloned.1.call-update
  294.8 0.0 reduce-scatter.5.cloned.1.call-start
  294.8 17.0 %all-gather.8.cloned.1.call-done = bf16[1024,2688]{0,1:T(8,128)(2,1)} async-done(((bf16[512,2688]{0,1:T(8,128)(2,1)}), bf16[1024,2688]{0,1:T(8,128)(2,1)}) %all-gather.8.cloned.1.call-update) | async-done | bytes 5505040 | tf_op jit(solution)/shard_map/all_gather | solution.py:77
  311.8 23.3 %fusion.3 = f32[1024,4096]{1,0:T(8,128)} fusion(bf16[4096,896]{0,1:T(8,128)(2,1)} %get-tuple-element.28, bf16[4096,896]{0,1:T(8,128)(2,1)} %get-tuple-element.29, bf16[1024,2688]{0,1:T(8,128)(2,1)} %all-gather.8.cloned.1.call-done), kind=kOutput, calls=%fused_computation.10 | convolution fusion | flops 15061745664 | bytes 35127296 | tf_op jit(solution)/shard_map/dot_general | solution.py:86
  335.2 13.4 %fusion.8 = f32[1024,4096]{1,0:T(8,128)S(1)} fusion(bf16[896,4096]{1,0:T(8,128)(2,1)} %param.15, bf16[112,8,32,128]{3,2,1,0:T(8,128)(2,1)} %bitcast.55, bf16[1024,2688]{0,1:T(8,128)(2,1)} %all-gather.8.cloned.1.call-done), kind=kOutput, calls=%fused_computation.20 | convolution fusion | flops 7519862784 | bytes 33292288 | tf_op jit(solution)/shard_map/dot_general | solution.py:85
  348.6 18.3 %pad_maximum_fusion = f32[1024,8192]{1,0:T(8,128)} fusion(f32[1024,4096]{1,0:T(8,128)} %fusion.3, f32[1024,4096]{1,0:T(8,128)S(1)} %fusion.8), kind=kLoop, calls=%fused_computation | loop fusion | flops 8388608 | bytes 67108864 | tf_op jit(solution)/shard_map/concatenate | solution.py:83
  367.0 0.0 reduce-scatter.5.cloned.1.call-update
  367.0 0.0 copy-start.4
  367.0 23.2 %convolution_bitcast_fusion = f32[4096,1792]{0,1:T(8,128)} fusion(bf16[1024,4096]{1,0:T(8,128)(2,1)} %all-gather.4.cloned.1.call-done, bf16[1024,2688]{0,1:T(8,128)(2,1)} %all-gather.8.cloned.1.call-done), kind=kOutput, calls=%fused_computation.1 | convolution fusion | flops 15032385536 | bytes 41418752 | tf_op jit(solution)/shard_map/dot_general | solution.py:96
  390.2 1.9 mul.122
  392.1 7.1 mul.119
  399.3 26.2 %fusion.1 = (bf16[4096,896]{0,1:T(8,128)(2,1)}, bf16[4096,896]{0,1:T(8,128)(2,1)}) fusion(f32[112,8,32,128]{3,2,1,0:T(8,128)S(1)} %bitcast.50, f32[4096,1792]{0,1:T(8,128)} %convolution_bitcast_fusion, f32[112,8,32,128]{3,2,1,0:T(8,128)} %bitcast.51), kind=kLoop, calls=%fused_computation.5 | loop fusion | flops 14680064 | bytes 73400320 | tf_op jit(solution)/shard_map/convert_element_type | solution.py:25
  425.5 10.9 %copy.23 = bf16[4096,896]{1,0:T(8,128)(2,1)} copy(bf16[4096,896]{0,1:T(8,128)(2,1)} %get-tuple-element.21) | data formatting | bytes 14680064
  436.4 10.8 %copy.22 = bf16[4096,896]{1,0:T(8,128)(2,1)} copy(bf16[4096,896]{0,1:T(8,128)(2,1)} %get-tuple-element.22) | data formatting | bytes 14680064
  447.2 7.1 mul.125
  454.3 24.6 %fusion = bf16[896,4096]{1,0:T(8,128)(2,1)} fusion(f32[112,8,32,128]{3,2,1,0:T(8,128)} %bitcast.58, bf16[1024,4096]{1,0:T(8,128)(2,1)} %all-gather.6.cloned.1.call-done, bf16[1024,2688]{0,1:T(8,128)(2,1)} %all-gather.8.cloned.1.call-done), kind=kOutput, calls=%fused_computation.3 | convolution fusion | flops 7523532800 | bytes 32243712 | tf_op jit(solution)/shard_map/dot_general | solution.py:100
  478.9 579.2 %reduce-scatter.5.cloned.1.call-done = f32[64,8192]{1,0:T(8,128)} async-done(((f32[1024,8192]{1,0:T(8,128)}), f32[64,8192]{1,0:T(8,128)}) %reduce-scatter.5.cloned.1.call-update) | async-done | bytes 2097168 | tf_op jit(solution)/shard_map/reduce_scatter | solution.py:82
  1058.2 1.7 convert.4
  1059.9 1.0 fusion.16
  (21 shorter events, 0.0 us)
Async XLA Ops:
  7.2 118.7 %all-gather.6.cloned.1.call-start = ((), (), s32[]{:S(2)}) async-start(), calls=%async_computation.3 | async-start | bytes 8912896 | tf_op jit(solution)/shard_map/all_gather | solution.py:60
  7.9 231.2 %all-gather.4.cloned.1.call-start = ((), (), s32[]{:S(2)}) async-start(), calls=%async_computation.2 | async-start | bytes 8912896 | tf_op jit(solution)/shard_map/all_gather | solution.py:59
  8.6 280.7 %reduce-scatter.3.cloned.1.call-start = ((), (), s32[]{:S(2)}) async-start(), calls=%async_computation.4 | async-start | bytes 16515072 | tf_op jit(solution)/shard_map/reduce_scatter | solution.py:62
  19.5 11.1 %copy-start.5 = (s32[32,7]{0,1:T(8,128)S(1)}, s32[32,7]{0,1:T(8,128)}, u32[]{:S(2)}) copy-start(s32[32,7]{0,1:T(8,128)} %param.19) | copy-start | bytes 2692
  19.5 11.1 %copy-start.6 = (s32[32,7]{0,1:T(8,128)S(1)}, s32[32,7]{0,1:T(8,128)}, u32[]{:S(2)}) copy-start(s32[32,7]{0,1:T(8,128)} %param.16) | copy-start | bytes 2692
  19.5 11.7 %copy-start.7 = (s32[32,7]{0,1:T(8,128)S(1)}, s32[32,7]{0,1:T(8,128)}, u32[]{:S(2)}) copy-start(s32[32,7]{0,1:T(8,128)} %param.20) | copy-start | bytes 2692
  19.5 11.7 %copy-start.8 = (s32[32,7]{0,1:T(8,128)S(1)}, s32[32,7]{0,1:T(8,128)}, u32[]{:S(2)}) copy-start(s32[32,7]{0,1:T(8,128)} %param.17) | copy-start | bytes 2692
  19.5 12.3 %copy-start.9 = (s32[7,32]{1,0:T(8,128)S(1)}, s32[7,32]{1,0:T(8,128)}, u32[]{:S(2)}) copy-start(s32[7,32]{1,0:T(8,128)} %param.21) | copy-start | bytes 2692
  19.5 12.3 %copy-start.10 = (s32[7,32]{1,0:T(8,128)S(1)}, s32[7,32]{1,0:T(8,128)}, u32[]{:S(2)}) copy-start(s32[7,32]{1,0:T(8,128)} %param.18) | copy-start | bytes 2692
  31.8 6.4 slice-start
  32.4 5.8 slice-start.1
  32.4 7.5 copy-start
  126.9 2.9 copy-start.1
  272.8 39.1 %all-gather.8.cloned.1.call-start = ((), (), s32[]{:S(2)}) async-start(), calls=%async_computation.5 | async-start | bytes 8257536 | tf_op jit(solution)/shard_map/all_gather | solution.py:77
  294.8 763.4 %reduce-scatter.5.cloned.1.call-start = ((), (), s32[]{:S(2)}) async-start(), calls=%async_computation.6 | async-start | bytes 35651584 | tf_op jit(solution)/shard_map/reduce_scatter | solution.py:82
  367.0 23.2 %copy-start.4 = (f32[32,7]{0,1:T(8,128)S(1)}, f32[32,7]{0,1:T(8,128)}, u32[]{:S(2)}) copy-start(f32[32,7]{0,1:T(8,128)} %get-tuple-element.20) | copy-start | bytes 2692
  390.2 1.9 copy-start.3
  436.4 10.8 %copy-start.2 = (f32[7,32]{1,0:T(8,128)S(1)}, f32[7,32]{1,0:T(8,128)}, u32[]{:S(2)}) copy-start(f32[7,32]{1,0:T(8,128)} %get-tuple-element.16) | copy-start | bytes 2692
Sparse Core Ops, SparseCore 0:
  10.8 115.0 all-gather.5
  128.6 110.4 all-gather.3
  272.9 16.3 reduce-scatter.2
  294.9 16.8 all-gather.7
  367.1 691.0 reduce-scatter.4
where the time goes:
time: 1080 us; the launch traced here: 1070 us
  waiting for transfers between devices  783 us (72%)
  matrix products  124 us (11%)
  other arithmetic  74.9 us (7%)
  local copies, waits for them, and re-layouts  72.2 us (7%)
  between operations  14.4 us (1%)
    reduce_scatter x1, waiting for transfers between devices, shards(): lax.psum_scatter(jnp.concatenate([jnp.dot(hidden_all, eff_down, preferred...  579 us
    all_gather x1, waiting for transfers between devices, shards(): lax.all_gather(tokens, ('col', 'depth'), axis=0, tiled=True)  93.1 us
    all_gather x1, waiting for transfers between devices, shards(): lax.all_gather(out_grad, ('col', 'depth'), axis=0, tiled=True)  75.3 us
    unnamed x30, local copies, waits for them, and re-layouts  48.2 us
    convert_element_type x1, other arithmetic, masked_grad(): return blocks.reshape(grad.shape).astype(jnp.bfloat16)  26.2 us
    dot_general x1, matrix products, shards(): jnp.dot(hidden_all.T, gathered_grad, preferred_element_type=jnp.float32)  24.6 us
    dot_general x1, matrix products, shards(): jnp.dot(pair_grad, paired.T, preferred_element_type=jnp.float32)  23.3 us
    dot_general x1, matrix products, shards(): jnp.dot(gathered_in.T, pair_grad, preferred_element_type=jnp.float32)  23.2 us
  transfers between devices with their start and end apart: 5, of which 5 were waited for; matrix products, arithmetic and copies ran while one was open for 16% of the time, Pallas kernels for 0%

commit v1 on v0

--- a/solution.py
+++ b/solution.py
@@ -2,6 +2,18 @@
 import jax.numpy as jnp
 from jax import lax
 from jax.sharding import PartitionSpec as P
+
+
+def collect(x, axis, dim):
+    ways, here = (lax.axis_size(axis), lax.axis_index(axis))
+    grown, reach = (x, 1)
+    while reach < ways:
+        theirs = lax.ppermute(grown, axis, [(d, d ^ reach) for d in range(ways)])
+        mine_first = jnp.concatenate([grown, theirs], axis=dim)
+        theirs_first = jnp.concatenate([theirs, grown], axis=dim)
+        grown = jnp.where(here & reach == 0, mine_first, theirs_first)
+        reach = 2 * reach
+    return grown
 
 
 def block_factor(keep, exps):
@@ -56,7 +68,7 @@
     width = gate_w.shape[1]
     paired = jnp.concatenate([eff_gate, eff_up], axis=1)
     gathered_in, gathered_grad = (
-        lax.all_gather(tokens, ("col", "depth"), axis=0, tiled=True),
+        collect(tokens, ("col", "depth"), 0),
         lax.all_gather(out_grad, ("col", "depth"), axis=0, tiled=True),
     )
     sums = lax.psum_scatter(

time: 1080 us -> 1140 us (1.056)
  local copies, waits for them, and re-layouts: 72.2 us -> 139 us
  waiting for transfers between devices: 783 us -> 766 us
    ppermute x0 -> x4, waiting for transfers between devices: none -> 213 us  [collect(): theirs = lax.ppermute(grown, axis, [(d, d ^ reach) for d in range(ways)])]
    all_gather x1 -> x0, waiting for transfers between devices: 93.1 us -> none  [shards(): lax.all_gather(tokens, ('col', 'depth'), axis=0, tiled=True)]
    all_gather x1, waiting for transfers between devices: 75.3 us -> 0.01 us  [shards(): lax.all_gather(out_grad, ('col', 'depth'), axis=0, tiled=True)]
    reduce_scatter x1, waiting for transfers between devices: 579 us -> 517 us  [shards(): lax.psum_scatter(jnp.concatenate([jnp.dot(hidden_all, eff_down, preferred...]
    mul x3 -> x5, local copies, waits for them, and re-layouts: 16.2 us -> 54.1 us  [masked_grad(): grad.reshape(rows, grad.shape[0] // rows, cols, grad.shape[1] // cols)]
    unnamed x30 -> x36, local copies, waits for them, and re-layouts: 48.2 us -> 77.2 us
  transfers between devices with their start and end apart: 5 -> 8, of which waited for: 5 -> 7; matrix products, arithmetic and copies ran while one was open for 16% -> 22% of each run, Pallas kernels for 0% -> 0%
where the time goes in v1:
time: 1140 us; the launch traced here: 1130 us
  waiting for transfers between devices  766 us (67%)
  local copies, waits for them, and re-layouts  139 us (12%)
  matrix products  125 us (11%)
  other arithmetic  80.3 us (7%)
  between operations  14.3 us (1%)
    reduce_scatter x1, waiting for transfers between devices, shards(): lax.psum_scatter(jnp.concatenate([jnp.dot(hidden_all, eff_down, preferred...  517 us
    ppermute x4, waiting for transfers between devices, collect(): theirs = lax.ppermute(grown, axis, [(d, d ^ reach) for d in range(ways)])  213 us
    unnamed x36, local copies, waits for them, and re-layouts  77.2 us
    mul x5, local copies, waits for them, and re-layouts, masked_grad(): grad.reshape(rows, grad.shape[0] // rows, cols, grad.shape[1] // cols)  54.1 us
    convert_element_type x1, other arithmetic, masked_grad(): return blocks.reshape(grad.shape).astype(jnp.bfloat16)  24.7 us
    dot_general x1, matrix products, shards(): jnp.dot(gathered_in.T, pair_grad, preferred_element_type=jnp.float32)  23.8 us
    dot_general x1, matrix products, shards(): jnp.dot(pair_grad, paired.T, preferred_element_type=jnp.float32)  23.1 us
  transfers between devices with their start and end apart: 8, of which 7 were waited for; matrix products, arithmetic and copies ran while one was open for 22% of the time, Pallas kernels for 0%

profile of v1, /device:TPU:0, one launch (start us, length us, event | category | flops | bytes accessed | tf_op | source)
XLA Modules:
  0.0 1133.7 jit_solution(312314134784099285)
XLA Ops:
  7.2 0.7 all-gather.3.cloned.1.call-update
  7.9 3.1 collective-permute-start
  11.1 12.1 %collective-permute-done = bf16[64,4096]{1,0:T(8,128)(2,1)S(1)} collective-permute-done((bf16[64,4096]{1,0:T(8,128)(2,1)}, bf16[64,4096]{1,0:T(8,128)(2,1)S(1)}, u32[]{:S(2)}, u32[]{:S(2)}) %collective-permute-start) | collective-permute-done | bytes 524320 | tf_op jit(solution)/shard_map/ppermute | solution.py:11
  23.2 1.4 maximum_select_fusion.5
  24.6 2.8 collective-permute-start.1
  27.5 76.9 %collective-permute-done.1 = bf16[128,4096]{1,0:T(8,128)(2,1)} collective-permute-done((bf16[128,4096]{1,0:T(8,128)(2,1)S(1)}, bf16[128,4096]{1,0:T(8,128)(2,1)}, u32[]{:S(2)}, u32[]{:S(2)}) %collective-permute-start.1) | collective-permute-done | bytes 1048608 | tf_op jit(solution)/shard_map/ppermute | solution.py:11
  104.4 2.3 maximum_select_fusion.2
  106.7 1.6 collective-permute-start.2
  108.3 75.6 %collective-permute-done.2 = bf16[256,4096]{1,0:T(8,128)(2,1)} collective-permute-done((bf16[256,4096]{1,0:T(8,128)(2,1)S(1)}, bf16[256,4096]{1,0:T(8,128)(2,1)}, u32[]{:S(2)}, u32[]{:S(2)}) %collective-permute-start.2) | collective-permute-done | bytes 2097184 | tf_op jit(solution)/shard_map/ppermute | solution.py:11
  183.9 4.6 maximum_select_fusion.1
  188.5 1.4 collective-permute-start.3
  189.9 10.8 copy.21
  200.7 10.8 copy.22
  211.5 0.6 fusion.15
  212.1 0.6 fusion.16
  212.7 0.6 fusion.14
  213.4 1.0 mul.108
  214.4 4.7 mul.104
  219.1 1.7 copy-done
  220.8 10.6 bitcast_multiply_fusion.2
  231.4 48.5 %collective-permute-done.3 = bf16[512,4096]{1,0:T(8,128)(2,1)} collective-permute-done((bf16[512,4096]{1,0:T(8,128)(2,1)}, bf16[512,4096]{1,0:T(8,128)(2,1)}, u32[]{:S(2)}, u32[]{:S(2)}) %collective-permute-start.3) | collective-permute-done | bytes 4194336 | tf_op jit(solution)/shard_map/ppermute | solution.py:11
  279.9 22.6 %fusion.4 = f32[1024,1792]{1,0:T(8,128)} fusion(bf16[4096,896]{0,1:T(8,128)(2,1)} %get-tuple-element.18, bf16[4096,896]{0,1:T(8,128)(2,1)} %get-tuple-element.19, bf16[512,4096]{1,0:T(8,128)(2,1)} %collective-permute-done.3, bf16[512,4096]{1,0:T(8,128)(2,1)} %maximum_select_fusion.1, pred[]{:T(512)S(6)} %eq.12), kind=kOutput, calls=%fused_computation.12 | convolution fusion | flops 15099494400 | bytes 30408704 | tf_op jit(solution)/shard_map/dot_general | solution.py:77
  302.6 1.0 mul.112
  303.6 2.9 copy-done.2
  306.5 18.7 %convolution_bitcast_fusion = f32[1024,896]{1,0:T(8,128)} fusion(bf16[1024,4096]{1,0:T(8,128)(2,1)} %all-gather.3.cloned.1.call-done, bf16[896,4096]{1,0:T(8,128)(2,1)} %param.15, bf16[112,8,32,128]{3,2,1,0:T(8,128)(2,1)S(1)} %bitcast.51), kind=kOutput, calls=%fused_computation.23 | convolution fusion | flops 7519862784 | bytes 26738688 | tf_op jit(solution)/shard_map/dot_general | solution.py:78
  325.2 9.1 pad_maximum_fusion.2
  334.3 0.0 all-gather.5.cloned.1.call-start
  334.4 17.8 %reduce-scatter.3.cloned.1.call-done = f32[512,2688]{1,0:T(8,128)} async-done(((f32[1024,2688]{1,0:T(8,128)}), f32[512,2688]{1,0:T(8,128)}) %reduce-scatter.3.cloned.1.call-update) | async-done | bytes 5505040 | tf_op jit(solution)/shard_map/reduce_scatter | solution.py:74
  352.2 3.6 multiply_convert_fusion.2
  355.8 1.7 pad_maximum_fusion.5
  357.6 17.0 %all-gather.5.cloned.1.call-done = bf16[1024,2688]{1,0:T(8,128)(2,1)} async-done(((bf16[512,2688]{1,0:T(8,128)(2,1)}), bf16[1024,2688]{1,0:T(8,128)(2,1)}) %all-gather.5.cloned.1.call-update) | async-done | bytes 5505040 | tf_op jit(solution)/shard_map/all_gather | solution.py:89
  374.6 23.1 %fusion.3 = f32[1024,4096]{1,0:T(8,128)} fusion(bf16[4096,896]{0,1:T(8,128)(2,1)} %get-tuple-element.18, bf16[4096,896]{0,1:T(8,128)(2,1)} %get-tuple-element.19, bf16[1024,2688]{1,0:T(8,128)(2,1)} %all-gather.5.cloned.1.call-done), kind=kOutput, calls=%fused_computation.11 | convolution fusion | flops 15061745664 | bytes 35127296 | tf_op jit(solution)/shard_map/dot_general | solution.py:98
  397.7 16.2 %fusion.8 = f32[1024,4096]{1,0:T(8,128)} fusion(bf16[896,4096]{1,0:T(8,128)(2,1)} %param.15, bf16[112,8,32,128]{3,2,1,0:T(8,128)(2,1)} %bitcast.52, bf16[1024,2688]{1,0:T(8,128)(2,1)} %all-gather.5.cloned.1.call-done), kind=kOutput, calls=%fused_computation.24 | convolution fusion | flops 7519862784 | bytes 33292288 | tf_op jit(solution)/shard_map/dot_general | solution.py:97
  413.9 18.8 %pad_maximum_fusion = f32[1024,8192]{1,0:T(8,128)} fusion(f32[1024,4096]{1,0:T(8,128)S(1)} %copy-done.1, f32[1024,4096]{1,0:T(8,128)} %fusion.8), kind=kLoop, calls=%fused_computation | loop fusion | flops 8388608 | bytes 67108864 | tf_op jit(solution)/shard_map/concatenate | solution.py:95
  432.8 0.7 copy-done.5
  433.4 7.6 mul.126
  441.0 25.1 %copy.41 = f32[112,8,32,128]{3,1,2,0:T(8,128)} copy(f32[112,8,32,128]{3,2,1,0:T(8,128)} %bitcast.44) | data formatting | bytes 29360128
  466.1 16.2 %copy.25 = f32[4096,896]{1,0:T(8,128)} copy(f32[4096,896]{0,1:T(8,128)} %bitcast.42) | data formatting | bytes 29360128 | tf_op jit(solution)/shard_map/mul | solution.py:34
  482.3 7.0 mul.123
  489.3 25.2 %copy.42 = f32[112,8,32,128]{3,1,2,0:T(8,128)} copy(f32[112,8,32,128]{3,2,1,0:T(8,128)} %bitcast.45) | data formatting | bytes 29360128
  514.5 16.2 %copy.24 = f32[4096,896]{1,0:T(8,128)} copy(f32[4096,896]{0,1:T(8,128)} %bitcast.43) | data formatting | bytes 29360128 | tf_op jit(solution)/shard_map/mul | solution.py:34
  530.7 7.1 mul.129
  537.8 20.7 %fusion = bf16[896,4096]{1,0:T(8,128)(2,1)} fusion(f32[112,8,32,128]{3,2,1,0:T(8,128)} %bitcast.46, bf16[1024,4096]{1,0:T(8,128)(2,1)} %all-gather.3.cloned.1.call-done, bf16[1024,2688]{1,0:T(8,128)(2,1)} %all-gather.5.cloned.1.call-done), kind=kOutput, calls=%fused_computation.2 | convolution fusion | flops 7523532800 | bytes 32243712 | tf_op jit(solution)/shard_map/dot_general | solution.py:112
  558.6 23.8 %fusion.5 = f32[4096,1792]{1,0:T(8,128)} fusion(bf16[1024,2688]{1,0:T(8,128)(2,1)S(1)} %bitcast.54, bf16[512,4096]{1,0:T(8,128)(2,1)} %collective-permute-done.3, bf16[512,4096]{1,0:T(8,128)(2,1)} %maximum_select_fusion.1, pred[]{:T(512)S(6)} %eq.12), kind=kOutput, calls=%fused_computation.18 | convolution fusion | flops 15070134272 | bytes 41418752 | tf_op jit(solution)/shard_map/dot_general | solution.py:108
  582.4 24.7 %fusion.1 = (bf16[4096,896]{1,0:T(8,128)(2,1)}, bf16[4096,896]{1,0:T(8,128)(2,1)}) fusion(f32[4096,896]{1,0:T(8,128)} %copy.25, f32[4096,1792]{1,0:T(8,128)} %fusion.5, f32[4096,896]{1,0:T(8,128)} %copy.24), kind=kLoop, calls=%fused_computation.6 | loop fusion | flops 14680064 | bytes 73400320 | tf_op jit(solution)/shard_map/convert_element_type | solution.py:37
  607.0 516.9 %reduce-scatter.5.cloned.1.call-done = f32[64,8192]{1,0:T(8,128)} async-done(((f32[1024,8192]{1,0:T(8,128)}), f32[64,8192]{1,0:T(8,128)}) %reduce-scatter.5.cloned.1.call-update) | async-done | bytes 2097168 | tf_op jit(solution)/shard_map/reduce_scatter | solution.py:94
  1123.9 1.7 convert.4
  1125.6 1.0 fusion.17
  (38 shorter events, 0.2 us)
Async XLA Ops:
  7.2 295.4 %all-gather.3.cloned.1.call-start = ((), (), s32[]{:S(2)}) async-start(), calls=%async_computation.2 | async-start | bytes 8912896 | tf_op jit(solution)/shard_map/all_gather | solution.py:72
  7.9 344.3 %reduce-scatter.3.cloned.1.call-start = ((), (), s32[]{:S(2)}) async-start(), calls=%async_computation.3 | async-start | bytes 16515072 | tf_op jit(solution)/shard_map/reduce_scatter | solution.py:74
  7.9 15.3 %collective-permute-start = (bf16[64,4096]{1,0:T(8,128)(2,1)}, bf16[64,4096]{1,0:T(8,128)(2,1)S(1)}, u32[]{:S(2)}, u32[]{:S(2)}) collective-permute-start(bf16[64,4096]{1,0:T(8,128)(2,1)} %param.11), channel_id=1, source_target_pairs={{0,1},{1,0},{2,3},{3,2},{4,5},{5,4},{6,7},{7,6},{8,9},{9,8},{10,11... | collective-permute-start | bytes 1572872 | tf_op jit(solution)/shard_map/ppermute | solution.py:11
  24.6 79.7 %collective-permute-start.1 = (bf16[128,4096]{1,0:T(8,128)(2,1)S(1)}, bf16[128,4096]{1,0:T(8,128)(2,1)}, u32[]{:S(2)}, u32[]{:S(2)}) collective-permute-start(bf16[128,4096]{1,0:T(8,128)(2,1)S(1)} %maximum_select_fusion.5), channel_id=1, source_target_pairs={{0,2},{1,3},{2,0},{3,1},{4,6},{5,7},{6,4},{7,5},{8,10},{9,11},{10,... | collective-permute-start | bytes 3145736 | tf_op jit(solution)/shard_map/ppermute | solution.py:11
  106.7 77.2 %collective-permute-start.2 = (bf16[256,4096]{1,0:T(8,128)(2,1)S(1)}, bf16[256,4096]{1,0:T(8,128)(2,1)}, u32[]{:S(2)}, u32[]{:S(2)}) collective-permute-start(bf16[256,4096]{1,0:T(8,128)(2,1)S(1)} %maximum_select_fusion.2), channel_id=1, source_target_pairs={{0,4},{1,5},{2,6},{3,7},{4,0},{5,1},{6,2},{7,3},{8,12},{9,13},{10,... | collective-permute-start | bytes 6291464 | tf_op jit(solution)/shard_map/ppermute | solution.py:11
  188.5 91.4 %collective-permute-start.3 = (bf16[512,4096]{1,0:T(8,128)(2,1)}, bf16[512,4096]{1,0:T(8,128)(2,1)}, u32[]{:S(2)}, u32[]{:S(2)}) collective-permute-start(bf16[512,4096]{1,0:T(8,128)(2,1)} %maximum_select_fusion.1), channel_id=1, source_target_pairs={{0,8},{1,9},{2,10},{3,11},{4,12},{5,13},{6,14},{7,15},{8,0},{9,1},... | collective-permute-start | bytes 12582920 | tf_op jit(solution)/shard_map/ppermute | solution.py:11
  200.6 10.9 copy-start.6
  200.6 10.9 copy-start.7
  200.7 11.5 %copy-start.8 = (s32[32,7]{0,1:T(8,128)S(1)}, s32[32,7]{0,1:T(8,128)}, u32[]{:S(2)}) copy-start(s32[32,7]{0,1:T(8,128)} %param.20) | copy-start | bytes 2692
  200.7 11.5 %copy-start.9 = (s32[32,7]{0,1:T(8,128)S(1)}, s32[32,7]{0,1:T(8,128)}, u32[]{:S(2)}) copy-start(s32[32,7]{0,1:T(8,128)} %param.17) | copy-start | bytes 2692
  200.7 12.1 %copy-start.10 = (s32[7,32]{1,0:T(8,128)S(1)}, s32[7,32]{1,0:T(8,128)}, u32[]{:S(2)}) copy-start(s32[7,32]{1,0:T(8,128)} %param.21) | copy-start | bytes 2692
  200.7 12.1 %copy-start.11 = (s32[7,32]{1,0:T(8,128)S(1)}, s32[7,32]{1,0:T(8,128)}, u32[]{:S(2)}) copy-start(s32[7,32]{1,0:T(8,128)} %param.18) | copy-start | bytes 2692
  212.7 6.4 slice-start
  213.4 5.8 slice-start.1
  213.4 7.5 copy-start
  303.6 2.9 copy-start.2
  334.3 40.3 %all-gather.5.cloned.1.call-start = ((), (), s32[]{:S(2)}) async-start(), calls=%async_computation.4 | async-start | bytes 8257536 | tf_op jit(solution)/shard_map/all_gather | solution.py:89
  357.5 766.4 %reduce-scatter.5.cloned.1.call-start = ((), (), s32[]{:S(2)}) async-start(), calls=%async_computation.5 | async-start | bytes 35651584 | tf_op jit(solution)/shard_map/reduce_scatter | solution.py:94
  397.7 16.2 %copy-start.1 = (f32[1024,4096]{1,0:T(8,128)S(1)}, f32[1024,4096]{1,0:T(8,128)}, u32[]{:S(2)}) copy-start(f32[1024,4096]{1,0:T(8,128)} %fusion.3) | copy-start | bytes 50331652
  432.7 0.7 copy-start.5
  466.1 16.2 %copy-start.4 = (f32[32,7]{0,1:T(8,128)S(1)}, f32[32,7]{0,1:T(8,128)}, u32[]{:S(2)}) copy-start(f32[32,7]{0,1:T(8,128)} %get-tuple-element.8) | copy-start | bytes 2692
  514.5 16.2 %copy-start.3 = (f32[7,32]{1,0:T(8,128)S(1)}, f32[7,32]{1,0:T(8,128)}, u32[]{:S(2)}) copy-start(f32[7,32]{1,0:T(8,128)} %get-tuple-element.6) | copy-start | bytes 2692
  530.7 27.8 %slice-start.2 = ((s8[5505024]{0:T(1024)(128)(4,1)}), s8[4194304]{0:T(1024)(128)(4,1)S(1)}, s32[]{:S(2)}) async-start(s8[5505024]{0:T(1024)(128)(4,1)} %bitcast.53), calls=%async_computation.8 | async-start | bytes 8388608
  537.8 20.7 %slice-start.3 = ((s8[5505024]{0:T(1024)(128)(4,1)}), s8[1310720]{0:T(1024)(128)(4,1)S(1)}, s32[]{:S(2)}) async-start(s8[5505024]{0:T(1024)(128)(4,1)} %bitcast.53), calls=%async_computation.9 | async-start | bytes 2621440
Sparse Core Ops, SparseCore 0:
  10.8 180.4 all-gather.2
  334.4 17.6 reduce-scatter.2
  357.7 16.8 all-gather.4
  432.9 691.0 reduce-scatter.4
